TPU v7x, 32 devices: a whole 2x2x4 slice. The times are simulated.
32 devices in a mesh: row: 4 (over z), col: 8 (over y, x, core).
Axes of the slice: x: 2, y: 2, z: 4, core: 2. Of those that a mesh axis runs over, the one named last changes fastest.
Arguments:
- slab: float32 [4096, 8192], P('row', 'col'), may hold values from -6 to 6
- owner: int32 [2], replicated, may hold values from 0 to 7, as said below
- leaf_reflectors: float32 [2, 4096, 2048], P(None, 'row', 'col'), may hold values from -0.1875 to 0.1875
- leaf_factors: float32 [2, 1024, 2048], P(None, 'row', 'col'), as said below
- tree_reflectors: float32 [2, 2, 1024, 256], P(None, None, 'row'), may hold values from -0.25 to 0.25
- tree_mixers: float32 [2, 2, 1024, 256], P(None, None, 'row'), may hold values from -0.1875 to 0.1875
Outputs:
- updated: float32 [4096, 8192], P('row', 'col')
Inputs may be any that keep to these rules, and one draw needn't show every extreme that they name: `owner`: the 2 owners are distinct column blocks, and one of them is the last column block. Every 256 x 256 block of leaf_factors is upper triangular with diagonal entries from 1 to 2.
All inputs are finite; a program needn't handle non-finite values.
Results may differ from a plain program's by a relative error of at most 0.00015.
Values sent between devices are 32-bit elements; how exact they have to be, the bound alone decides.
No kernel may reach another device: no remote copies, remote signals or barrier semaphores. Data moves between devices by JAX's collectives and lax.ppermute only.
A program may use at most 64 MiB of HBM per device.

v0:
```python
import jax
import jax.numpy as jnp
from jax import lax
from jax.sharding import PartitionSpec as P

HIGH = lax.Precision.HIGHEST
LEADING = (((0,), (0,)), ((), ()))


def from_partner(shard, axis, apart):
    return lax.ppermute(shard, axis, [(i, i ^ 1 << apart) for i in range(lax.axis_size(axis))])


def apply_leaf(matrix, received, first_row, rows_dev):
    reflect_rows = received[first_row:rows_dev]
    factor_block = received[rows_dev:]
    lower = matrix[first_row:]
    projected = lax.dot_general(
        reflect_rows, lower, LEADING, precision=HIGH, preferred_element_type=jnp.float32
    )
    scaled = lax.dot_general(
        factor_block, projected, LEADING, precision=HIGH, preferred_element_type=jnp.float32
    )
    lower = lower - jnp.dot(
        reflect_rows, scaled, precision=HIGH, preferred_element_type=jnp.float32
    )
    return jnp.concatenate([matrix[:first_row], lower], axis=0)


def tree_step(matrix, halves, mixers, first_row, width, levels):
    top_rows = matrix[first_row : first_row + width]
    for level_no in range(levels):
        partial_sum = lax.dot_general(
            halves[level_no], top_rows, LEADING, precision=HIGH, preferred_element_type=jnp.float32
        )
        partner_sum = from_partner(partial_sum, "row", level_no)
        top_rows = top_rows - jnp.dot(
            mixers[level_no],
            partial_sum + partner_sum,
            precision=HIGH,
            preferred_element_type=jnp.float32,
        )
    return lax.dynamic_update_slice_in_dim(matrix, top_rows, first_row, 0)


def shards(slab, owner, leaf_reflectors, leaf_factors, tree_reflectors, tree_mixers):
    rows_dev = slab.shape[0]
    width = leaf_factors.shape[1]
    panels = owner.shape[0]
    levels = lax.axis_size("row").bit_length() - 1
    is_owner = (lax.axis_index("col") == owner).astype(jnp.float32)
    stacked = jnp.concatenate([leaf_reflectors, leaf_factors], axis=1) * is_owner[:, None, None]
    received = lax.psum(stacked, "col")
    panel_blocks = [received[panel_no] for panel_no in range(panels)]
    matrix = slab
    for panel_no in range(panels):
        matrix = apply_leaf(matrix, panel_blocks[panel_no], panel_no * width, rows_dev)
        matrix = tree_step(
            matrix,
            tree_reflectors[panel_no],
            tree_mixers[panel_no],
            panel_no * width,
            width,
            levels,
        )
    return matrix


def solution(mesh):
    return jax.shard_map(
        shards,
        mesh=mesh,
        in_specs=(
            P("row", "col"),
            P(),
            P(None, "row", "col"),
            P(None, "row", "col"),
            P(None, None, "row", None),
            P(None, None, "row", None),
        ),
        out_specs=P("row", "col"),
        check_vma=False,
    )
```

profile of v0, /device:TPU:0, one launch (start us, length us, event | category | flops | bytes accessed | tf_op | source)
XLA Modules:
  0.0 220.8 jit_solution(15570357751311416546)
XLA Ops:
  6.5 0.7 compare_convert_fusion
  7.2 3.5 %maximum_multiply_fusion = f32[2,1280,256]{2,1,0:T(8,128)} fusion(f32[2,256,256]{2,1,0:T(8,128)} %param.9, f32[2,1024,256]{2,1,0:T(8,128)} %param.8, f32[2]{0:T(128)S(1)} %compare_convert_fusion), kind=kLoop, calls=%fused_computation.4 | loop fusion | flops 1310720 | bytes 5242888 | tf_op jit(solution)/shard_map/mul | solution.py:52
  10.7 67.5 %all-reduce.2.cloned.1.call-done = f32[2,1280,256]{2,1,0:T(8,128)} async-done(((f32[2,1280,256]{2,1,0:T(8,128)}), f32[2,1280,256]{2,1,0:T(8,128)}) %all-reduce.2.cloned.1.call-update) | async-done | bytes 2621456 | tf_op jit(solution)/shard_map/psum | solution.py:53
  78.2 6.2 %fusion.11 = f32[256,1024]{1,0:T(8,128)S(1)} fusion(f32[1024,1024]{1,0:T(8,128)} %param.6, f32[2,1280,256]{2,1,0:T(8,128)} %all-reduce.2.cloned.1.call-done), kind=kOutput, calls=%fused_computation.24 | convolution fusion | flops 3221225472 | bytes 6291456 | tf_op jit(solution)/shard_map/dot_general | solution.py:18
  84.4 2.0 fusion.15
  86.4 3.8 %convolution_subtract_fusion = f32[1024,1024]{1,0:T(8,128)S(1)} fusion(f32[1024,1024]{1,0:T(8,128)S(1)} %copy-done, f32[256,1024]{1,0:T(8,128)S(1)} %fusion.15, f32[2,1280,256]{2,1,0:T(8,128)S(1)} %copy-done.1), kind=kOutput, calls=%fused_computation.5 | convolution fusion | flops 3222274048 | bytes 10485760 | tf_op jit(solution)/shard_map/dot_general | solution.py:24
  90.2 1.9 convolution_bitcast_fusion.7
  92.1 1.6 collective-permute-start
  93.7 2.7 %fusion = f32[256,1024]{1,0:T(8,128)S(1)} fusion(f32[1024,1024]{1,0:T(8,128)S(1)} %convolution_subtract_fusion, f32[2,1280,256]{2,1,0:T(8,128)S(1)} %copy-done.1), kind=kOutput, calls=%fused_computation.2 | convolution fusion | flops 2415919104 | bytes 4980736 | tf_op jit(solution)/shard_map/dot_general | solution.py:18
  96.4 1.0 fusion.14
  97.5 3.0 %slice_subtract_fusion = f32[768,1024]{1,0:T(8,128)S(1)} fusion(f32[1024,1024]{1,0:T(8,128)S(1)} %convolution_subtract_fusion, f32[256,1024]{1,0:T(8,128)S(1)} %fusion.14, f32[2,1280,256]{2,1,0:T(8,128)S(1)} %copy-done.1), kind=kOutput, calls=%fused_computation.1 | convolution fusion | flops 2416705536 | bytes 8126464 | tf_op jit(solution)/shard_map/dot_general | solution.py:24
  100.5 1.8 convolution_bitcast_fusion.3
  102.9 15.4 %collective-permute-done = f32[256,1024]{0,1:T(8,128)S(1)} collective-permute-done((f32[256,1024]{0,1:T(8,128)S(1)}, f32[256,1024]{0,1:T(8,128)S(1)}, u32[]{:S(2)}, u32[]{:S(2)}) %collective-permute-start) | collective-permute-done | bytes 1048608 | tf_op jit(solution)/shard_map/ppermute | solution.py:11
  118.3 1.2 fusion.2
  119.4 1.9 convolution_bitcast_fusion.5
  121.3 2.5 %collective-permute-start.1 = (f32[256,1024]{0,1:T(8,128)S(1)}, f32[256,1024]{0,1:T(8,128)S(1)}, u32[]{:S(2)}, u32[]{:S(2)}) collective-permute-start(f32[256,1024]{0,1:T(8,128)S(1)} %convolution_bitcast_fusion.5), channel_id=1, source_target_pairs={{0,16},{8,24},{16,0},{24,8},{1,17},{9,25},{17,1},{25,9},{2,18},{10... | collective-permute-start | bytes 3145736 | tf_op jit(solution)/shard_map/ppermute | solution.py:11
  123.8 34.6 %collective-permute-done.2 = f32[256,1024]{0,1:T(8,128)S(1)} collective-permute-done((f32[256,1024]{0,1:T(8,128)S(1)}, f32[256,1024]{0,1:T(8,128)S(1)}, u32[]{:S(2)}, u32[]{:S(2)}) %collective-permute-start.2) | collective-permute-done | bytes 1048608 | tf_op jit(solution)/shard_map/ppermute | solution.py:11
  158.4 1.1 fusion.4
  159.5 1.8 convolution_bitcast_fusion.1
  161.4 31.2 %collective-permute-done.1 = f32[256,1024]{0,1:T(8,128)S(1)} collective-permute-done((f32[256,1024]{0,1:T(8,128)S(1)}, f32[256,1024]{0,1:T(8,128)S(1)}, u32[]{:S(2)}, u32[]{:S(2)}) %collective-permute-start.1) | collective-permute-done | bytes 1048608 | tf_op jit(solution)/shard_map/ppermute | solution.py:11
  192.6 1.2 fusion.3
  193.8 2.6 %pad_maximum_fusion = f32[1024,1024]{1,0:T(8,128)} fusion(f32[768,1024]{1,0:T(8,128)S(1)} %slice_subtract_fusion, f32[256,1024]{1,0:T(8,128)S(1)} %fusion.3), kind=kLoop, calls=%fused_computation | loop fusion | flops 1048576 | bytes 8388608 | tf_op jit(solution)/shard_map/concatenate | solution.py:27
  196.4 15.4 %collective-permute-done.3 = f32[256,1024]{0,1:T(8,128)S(1)} collective-permute-done((f32[256,1024]{0,1:T(8,128)S(1)}, f32[256,1024]{0,1:T(8,128)S(1)}, u32[]{:S(2)}, u32[]{:S(2)}) %collective-permute-start.3) | collective-permute-done | bytes 1048608 | tf_op jit(solution)/shard_map/ppermute | solution.py:11
  211.9 2.1 fusion.6
  (12 shorter events, 0.7 us)
Async XLA Ops:
  6.5 71.7 %all-reduce.2.cloned.1.call-start = ((), (), s32[]{:S(2)}) async-start(), calls=%async_computation | async-start | bytes 5242880 | tf_op jit(solution)/shard_map/psum | solution.py:53
  78.2 8.2 %copy-start = (f32[1024,1024]{1,0:T(8,128)S(1)}, f32[1024,1024]{1,0:T(8,128)}, u32[]{:S(2)}) copy-start(f32[1024,1024]{1,0:T(8,128)} %param.6) | copy-start | bytes 12582916
  78.2 8.2 %copy-start.1 = (f32[2,1280,256]{2,1,0:T(8,128)S(1)}, f32[2,1280,256]{2,1,0:T(8,128)}, u32[]{:S(2)}) copy-start(f32[2,1280,256]{2,1,0:T(8,128)} %all-reduce.2.cloned.1.call-done) | copy-start | bytes 7864324
  86.4 3.8 %copy-start.2 = (f32[2,2,256,256]{3,2,1,0:T(8,128)S(1)}, f32[2,2,256,256]{3,2,1,0:T(8,128)}, u32[]{:S(2)}) copy-start(f32[2,2,256,256]{3,2,1,0:T(8,128)} %param.10) | copy-start | bytes 3145732
  92.1 26.2 %collective-permute-start = (f32[256,1024]{0,1:T(8,128)S(1)}, f32[256,1024]{0,1:T(8,128)S(1)}, u32[]{:S(2)}, u32[]{:S(2)}) collective-permute-start(f32[256,1024]{0,1:T(8,128)S(1)} %convolution_bitcast_fusion.7), channel_id=1, source_target_pairs={{0,8},{8,0},{16,24},{24,16},{1,9},{9,1},{17,25},{25,17},{2,10},{10... | collective-permute-start | bytes 3145736 | tf_op jit(solution)/shard_map/ppermute | solution.py:11
  97.4 20.8 %copy-start.3 = (f32[2,2,256,256]{3,2,1,0:T(8,128)S(1)}, f32[2,2,256,256]{3,2,1,0:T(8,128)}, u32[]{:S(2)}) copy-start(f32[2,2,256,256]{3,2,1,0:T(8,128)} %param.11) | copy-start | bytes 3145732
  102.3 56.1 %collective-permute-start.2 = (f32[256,1024]{0,1:T(8,128)S(1)}, f32[256,1024]{0,1:T(8,128)S(1)}, u32[]{:S(2)}, u32[]{:S(2)}) collective-permute-start(f32[256,1024]{0,1:T(8,128)S(1)} %convolution_bitcast_fusion.3), channel_id=1, source_target_pairs={{0,8},{8,0},{16,24},{24,16},{1,9},{9,1},{17,25},{25,17},{2,10},{10... | collective-permute-start | bytes 3145736 | tf_op jit(solution)/shard_map/ppermute | solution.py:11
  121.3 71.3 %collective-permute-start.1 = (f32[256,1024]{0,1:T(8,128)S(1)}, f32[256,1024]{0,1:T(8,128)S(1)}, u32[]{:S(2)}, u32[]{:S(2)}) collective-permute-start(f32[256,1024]{0,1:T(8,128)S(1)} %convolution_bitcast_fusion.5), channel_id=1, source_target_pairs={{0,16},{8,24},{16,0},{24,8},{1,17},{9,25},{17,1},{25,9},{2,18},{10... | collective-permute-start | bytes 3145736 | tf_op jit(solution)/shard_map/ppermute | solution.py:11
  161.3 50.5 %collective-permute-start.3 = (f32[256,1024]{0,1:T(8,128)S(1)}, f32[256,1024]{0,1:T(8,128)S(1)}, u32[]{:S(2)}, u32[]{:S(2)}) collective-permute-start(f32[256,1024]{0,1:T(8,128)S(1)} %convolution_bitcast_fusion.1), channel_id=1, source_target_pairs={{0,16},{8,24},{16,0},{24,8},{1,17},{9,25},{17,1},{25,9},{2,18},{10... | collective-permute-start | bytes 3145736 | tf_op jit(solution)/shard_map/ppermute | solution.py:11
Sparse Core Ops, SparseCore 0:
  10.8 67.3 all-reduce.1
where the time goes:
time: 221 us
  waiting for transfers between devices  164 us (74%)
  matrix products  31.7 us (14%)
  between operations  13.5 us (6%)
  other arithmetic  6.76 us (3%)
  starting transfers between devices  4.7 us (2%)
    ppermute x4, waiting for transfers between devices, from_partner(): lax.ppermute(shard, axis, [(i, i ^ 1 << apart) for i in range(lax.axis_si...  96.6 us
    psum x1, waiting for transfers between devices, shards(): received = lax.psum(stacked, 'col')  67.5 us
    dot_general x2, matrix products, apply_leaf(): lax.dot_general(reflect_rows, lower, LEADING, precision=HIGH, preferred_e...  8.91 us
    dot_general x4, matrix products, tree_step(): lax.dot_general(halves[level_no], top_rows, LEADING, precision=HIGH, pref...  7.35 us
    dot_general x2, matrix products, apply_leaf(): jnp.dot(reflect_rows, scaled, precision=HIGH, preferred_element_type=jnp....  6.81 us
    dot_general x4, matrix products, tree_step(): jnp.dot(mixers[level_no], partial_sum + partner_sum, precision=HIGH, pref...  5.55 us
    ppermute x4, starting transfers between devices, from_partner(): lax.ppermute(shard, axis, [(i, i ^ 1 << apart) for i in range(lax.axis_si...  4.69 us
  transfers between devices with their start and end apart: 5, of which 5 were waited for; matrix products, arithmetic and copies ran while one was open for 8% of the time, Pallas kernels for 0%

commit v1 on v0

--- a/solution.py
+++ b/solution.py
@@ -5,6 +5,14 @@
 
 HIGH = lax.Precision.HIGHEST
 LEADING = (((0,), (0,)), ((), ()))
+
+
+def sum_by_hops(x, axis):
+    peers, total = (lax.axis_size(axis), x)
+    for reach in [1 << k for k in range(peers.bit_length() - 1)]:
+        swap = [(i, i ^ reach) for i in range(peers)]
+        total = total + lax.ppermute(total, axis, swap)
+    return total
 
 
 def from_partner(shard, axis, apart):
@@ -50,7 +58,7 @@
     levels = lax.axis_size("row").bit_length() - 1
     is_owner = (lax.axis_index("col") == owner).astype(jnp.float32)
     stacked = jnp.concatenate([leaf_reflectors, leaf_factors], axis=1) * is_owner[:, None, None]
-    received = lax.psum(stacked, "col")
+    received = sum_by_hops(stacked, "col")
     panel_blocks = [received[panel_no] for panel_no in range(panels)]
     matrix = slab
     for panel_no in range(panels):

time: 221 us -> 262 us (1.19)
  waiting for transfers between devices: 164 us -> 217 us
  between operations: 13.5 us -> 0.17 us
  starting transfers between devices: 4.7 us -> 10.1 us
  matrix products: 31.7 us -> 28.4 us
    ppermute x0 -> x3, waiting for transfers between devices: none -> 118 us  [sum_by_hops(): total = total + lax.ppermute(total, axis, swap)]
    psum x1 -> x0, waiting for transfers between devices: 67.5 us -> none  [shards(): received = lax.psum(stacked, 'col')]
    ppermute x0 -> x3, starting transfers between devices: none -> 5.28 us  [sum_by_hops(): total = total + lax.ppermute(total, axis, swap)]
  transfers between devices with their start and end apart: 5 -> 7, of which waited for: 5 -> 7; matrix products, arithmetic and copies ran while one was open for 8% -> 6% of each run, Pallas kernels for 0% -> 0%
where the time goes in v1:
time: 262 us
  waiting for transfers between devices  217 us (83%)
  matrix products  28.4 us (11%)
  starting transfers between devices  10.1 us (4%)
  other arithmetic  6.28 us (2%)
    ppermute x3, waiting for transfers between devices, sum_by_hops(): total = total + lax.ppermute(total, axis, swap)  118 us
    ppermute x4, waiting for transfers between devices, from_partner(): lax.ppermute(shard, axis, [(i, i ^ 1 << apart) for i in range(lax.axis_si...  98.8 us
    dot_general x4, matrix products, tree_step(): lax.dot_general(halves[level_no], top_rows, LEADING, precision=HIGH, pref...  7.57 us
    dot_general x2, matrix products, apply_leaf(): lax.dot_general(reflect_rows, lower, LEADING, precision=HIGH, preferred_e...  6.62 us
    dot_general x2, matrix products, apply_leaf(): jnp.dot(reflect_rows, scaled, precision=HIGH, preferred_element_type=jnp....  6.56 us
    dot_general x4, matrix products, tree_step(): jnp.dot(mixers[level_no], partial_sum + partner_sum, precision=HIGH, pref...  5.55 us
    ppermute x3, starting transfers between devices, sum_by_hops(): total = total + lax.ppermute(total, axis, swap)  5.28 us
  transfers between devices with their start and end apart: 7, of which 7 were waited for; matrix products, arithmetic and copies ran while one was open for 6% of the time, Pallas kernels for 0%

profile of v1, /device:TPU:0, one launch (start us, length us, event | category | flops | bytes accessed | tf_op | source)
XLA Modules:
  0.0 262.0 jit_solution(15208589050875021806)
XLA Ops:
  0.7 2.0 maximum_multiply_fusion
  3.2 4.5 %collective-permute-done = f32[2,1280,256]{2,1,0:T(8,128)S(1)} collective-permute-done((f32[2,1280,256]{2,1,0:T(8,128)S(1)}, f32[2,1280,256]{2,1,0:T(8,128)S(1)}, u32[]{:S(2)}, u32[]{:S(2)}) %collective-permute-start) | collective-permute-done | bytes 2621472 | tf_op jit(solution)/shard_map/ppermute | solution.py:14
  8.1 2.9 %collective-permute-start.1 = (f32[2,1280,256]{2,1,0:T(8,128)S(1)}, f32[2,1280,256]{2,1,0:T(8,128)S(1)}, u32[]{:S(2)}, u32[]{:S(2)}) collective-permute-start(f32[2,1280,256]{2,1,0:T(8,128)S(1)} %add.21), channel_id=1, source_target_pairs={{0,2},{1,3},{2,0},{3,1},{4,6},{5,7},{6,4},{7,5},{8,10},{9,11},{10,... | collective-permute-start | bytes 7864328 | tf_op jit(solution)/shard_map/ppermute | solution.py:14
  11.0 57.2 %collective-permute-done.1 = f32[2,1280,256]{2,1,0:T(8,128)S(1)} collective-permute-done((f32[2,1280,256]{2,1,0:T(8,128)S(1)}, f32[2,1280,256]{2,1,0:T(8,128)S(1)}, u32[]{:S(2)}, u32[]{:S(2)}) %collective-permute-start.1) | collective-permute-done | bytes 2621472 | tf_op jit(solution)/shard_map/ppermute | solution.py:14
  68.5 1.8 collective-permute-start.2
  70.3 56.6 %collective-permute-done.2 = f32[2,1280,256]{2,1,0:T(8,128)S(1)} collective-permute-done((f32[2,1280,256]{2,1,0:T(8,128)S(1)}, f32[2,1280,256]{2,1,0:T(8,128)S(1)}, u32[]{:S(2)}, u32[]{:S(2)}) %collective-permute-start.2) | collective-permute-done | bytes 2621472 | tf_op jit(solution)/shard_map/ppermute | solution.py:14
  127.3 3.7 %fusion.11 = f32[256,1024]{1,0:T(8,128)S(1)} fusion(f32[1024,1024]{1,0:T(8,128)S(1)} %copy-done, f32[2,1280,256]{2,1,0:T(8,128)S(1)} %add.23), kind=kOutput, calls=%fused_computation.24 | convolution fusion | flops 3221225472 | bytes 6291456 | tf_op jit(solution)/shard_map/dot_general | solution.py:26
  132.1 3.8 %convolution_subtract_fusion = f32[1024,1024]{1,0:T(8,128)S(1)} fusion(f32[1024,1024]{1,0:T(8,128)S(1)} %copy-done, f32[256,1024]{1,0:T(8,128)S(1)} %fusion.15, f32[2,1280,256]{2,1,0:T(8,128)S(1)} %add.23), kind=kOutput, calls=%fused_computation.5 | convolution fusion | flops 3222274048 | bytes 10485760 | tf_op jit(solution)/shard_map/dot_general | solution.py:32
  135.9 2.9 %fusion = f32[256,1024]{1,0:T(8,128)S(1)} fusion(f32[1024,1024]{1,0:T(8,128)S(1)} %convolution_subtract_fusion, f32[2,1280,256]{2,1,0:T(8,128)S(1)} %add.23), kind=kOutput, calls=%fused_computation.2 | convolution fusion | flops 2415919104 | bytes 4980736 | tf_op jit(solution)/shard_map/dot_general | solution.py:26
  139.9 1.9 convolution_bitcast_fusion.7
  141.8 1.6 collective-permute-start.3
  143.3 2.8 %slice_subtract_fusion = f32[768,1024]{1,0:T(8,128)S(1)} fusion(f32[1024,1024]{1,0:T(8,128)S(1)} %convolution_subtract_fusion, f32[256,1024]{1,0:T(8,128)S(1)} %fusion.14, f32[2,1280,256]{2,1,0:T(8,128)S(1)} %add.23), kind=kOutput, calls=%fused_computation.1 | convolution fusion | flops 2416705536 | bytes 8126464 | tf_op jit(solution)/shard_map/dot_general | solution.py:32
  146.1 1.8 convolution_bitcast_fusion.3
  148.5 19.4 %collective-permute-done.3 = f32[256,1024]{0,1:T(8,128)S(1)} collective-permute-done((f32[256,1024]{0,1:T(8,128)S(1)}, f32[256,1024]{0,1:T(8,128)S(1)}, u32[]{:S(2)}, u32[]{:S(2)}) %collective-permute-start.3) | collective-permute-done | bytes 1048608 | tf_op jit(solution)/shard_map/ppermute | solution.py:19
  167.9 1.2 fusion.2
  169.1 1.9 convolution_bitcast_fusion.5
  171.0 2.6 collective-permute-start.4
  173.5 34.3 %collective-permute-done.5 = f32[256,1024]{0,1:T(8,128)S(1)} collective-permute-done((f32[256,1024]{0,1:T(8,128)S(1)}, f32[256,1024]{0,1:T(8,128)S(1)}, u32[]{:S(2)}, u32[]{:S(2)}) %collective-permute-start.5) | collective-permute-done | bytes 1048608 | tf_op jit(solution)/shard_map/ppermute | solution.py:19
  209.0 2.0 convolution_bitcast_fusion.1
  211.1 29.0 %collective-permute-done.4 = f32[256,1024]{0,1:T(8,128)S(1)} collective-permute-done((f32[256,1024]{0,1:T(8,128)S(1)}, f32[256,1024]{0,1:T(8,128)S(1)}, u32[]{:S(2)}, u32[]{:S(2)}) %collective-permute-start.4) | collective-permute-done | bytes 1048608 | tf_op jit(solution)/shard_map/ppermute | solution.py:19
  240.1 1.2 fusion.3
  241.3 2.6 pad_maximum_fusion
  243.9 16.0 %collective-permute-done.6 = f32[256,1024]{0,1:T(8,128)S(1)} collective-permute-done((f32[256,1024]{0,1:T(8,128)S(1)}, f32[256,1024]{0,1:T(8,128)S(1)}, u32[]{:S(2)}, u32[]{:S(2)}) %collective-permute-start.6) | collective-permute-done | bytes 1048608 | tf_op jit(solution)/shard_map/ppermute | solution.py:19
  260.0 2.1 fusion.6
  (16 shorter events, 6.1 us)
Async XLA Ops:
  2.7 5.1 %collective-permute-start = (f32[2,1280,256]{2,1,0:T(8,128)S(1)}, f32[2,1280,256]{2,1,0:T(8,128)S(1)}, u32[]{:S(2)}, u32[]{:S(2)}) collective-permute-start(f32[2,1280,256]{2,1,0:T(8,128)S(1)} %maximum_multiply_fusion), channel_id=1, source_target_pairs={{0,1},{1,0},{2,3},{3,2},{4,5},{5,4},{6,7},{7,6},{8,9},{9,8},{10,11... | collective-permute-start | bytes 7864328 | tf_op jit(solution)/shard_map/ppermute | solution.py:14
  8.1 60.1 %collective-permute-start.1 = (f32[2,1280,256]{2,1,0:T(8,128)S(1)}, f32[2,1280,256]{2,1,0:T(8,128)S(1)}, u32[]{:S(2)}, u32[]{:S(2)}) collective-permute-start(f32[2,1280,256]{2,1,0:T(8,128)S(1)} %add.21), channel_id=1, source_target_pairs={{0,2},{1,3},{2,0},{3,1},{4,6},{5,7},{6,4},{7,5},{8,10},{9,11},{10,... | collective-permute-start | bytes 7864328 | tf_op jit(solution)/shard_map/ppermute | solution.py:14
  68.5 58.8 %copy-start = (f32[1024,1024]{1,0:T(8,128)S(1)}, f32[1024,1024]{1,0:T(8,128)}, u32[]{:S(2)}) copy-start(f32[1024,1024]{1,0:T(8,128)} %param.6) | copy-start | bytes 12582916
  68.5 58.5 %collective-permute-start.2 = (f32[2,1280,256]{2,1,0:T(8,128)S(1)}, f32[2,1280,256]{2,1,0:T(8,128)S(1)}, u32[]{:S(2)}, u32[]{:S(2)}) collective-permute-start(f32[2,1280,256]{2,1,0:T(8,128)S(1)} %add.22), channel_id=1, source_target_pairs={{0,4},{1,5},{2,6},{3,7},{4,0},{5,1},{6,2},{7,3},{8,12},{9,13},{10,... | collective-permute-start | bytes 7864328 | tf_op jit(solution)/shard_map/ppermute | solution.py:14
  135.9 4.0 %copy-start.1 = (f32[2,2,256,256]{3,2,1,0:T(8,128)S(1)}, f32[2,2,256,256]{3,2,1,0:T(8,128)}, u32[]{:S(2)}) copy-start(f32[2,2,256,256]{3,2,1,0:T(8,128)} %param.10) | copy-start | bytes 3145732
  141.7 26.2 %copy-start.2 = (f32[2,2,256,256]{3,2,1,0:T(8,128)S(1)}, f32[2,2,256,256]{3,2,1,0:T(8,128)}, u32[]{:S(2)}) copy-start(f32[2,2,256,256]{3,2,1,0:T(8,128)} %param.11) | copy-start | bytes 3145732
  141.8 26.2 %collective-permute-start.3 = (f32[256,1024]{0,1:T(8,128)S(1)}, f32[256,1024]{0,1:T(8,128)S(1)}, u32[]{:S(2)}, u32[]{:S(2)}) collective-permute-start(f32[256,1024]{0,1:T(8,128)S(1)} %convolution_bitcast_fusion.7), channel_id=1, source_target_pairs={{0,8},{8,0},{16,24},{24,16},{1,9},{9,1},{17,25},{25,17},{2,10},{10... | collective-permute-start | bytes 3145736 | tf_op jit(solution)/shard_map/ppermute | solution.py:19
  147.9 59.9 %collective-permute-start.5 = (f32[256,1024]{0,1:T(8,128)S(1)}, f32[256,1024]{0,1:T(8,128)S(1)}, u32[]{:S(2)}, u32[]{:S(2)}) collective-permute-start(f32[256,1024]{0,1:T(8,128)S(1)} %convolution_bitcast_fusion.3), channel_id=1, source_target_pairs={{0,8},{8,0},{16,24},{24,16},{1,9},{9,1},{17,25},{25,17},{2,10},{10... | collective-permute-start | bytes 3145736 | tf_op jit(solution)/shard_map/ppermute | solution.py:19
  171.0 69.2 %collective-permute-start.4 = (f32[256,1024]{0,1:T(8,128)S(1)}, f32[256,1024]{0,1:T(8,128)S(1)}, u32[]{:S(2)}, u32[]{:S(2)}) collective-permute-start(f32[256,1024]{0,1:T(8,128)S(1)} %convolution_bitcast_fusion.5), channel_id=1, source_target_pairs={{0,16},{8,24},{16,0},{24,8},{1,17},{9,25},{17,1},{25,9},{2,18},{10... | collective-permute-start | bytes 3145736 | tf_op jit(solution)/shard_map/ppermute | solution.py:19
  211.0 48.9 %collective-permute-start.6 = (f32[256,1024]{0,1:T(8,128)S(1)}, f32[256,1024]{0,1:T(8,128)S(1)}, u32[]{:S(2)}, u32[]{:S(2)}) collective-permute-start(f32[256,1024]{0,1:T(8,128)S(1)} %convolution_bitcast_fusion.1), channel_id=1, source_target_pairs={{0,16},{8,24},{16,0},{24,8},{1,17},{9,25},{17,1},{25,9},{2,18},{10... | collective-permute-start | bytes 3145736 | tf_op jit(solution)/shard_map/ppermute | solution.py:19
